TPU v7x, 32 devices: a whole 2x2x4 slice. The times are simulated.
32 devices in a mesh: row: 8 (over z, y), feat: 4 (over x, core).
Axes of the slice: x: 2, y: 2, z: 4, core: 2. Of those that a mesh axis runs over, the one named last changes fastest.
Arguments:
- design: bfloat16 [1024, 65536], P('row', 'feat'), may hold values from -0.0234375 to 0.0234375
- targets: bfloat16 [1024, 48], P('row'), may hold values from -6 to 6
- factor: float32 [65536, 256], P(('feat', 'row')), may hold values from -0.09375 to 0.09375
- weights: float32 [256], replicated, may hold values from 0.3 to 3
- penalty: float32 [48], replicated, may hold values from 0.05 to 0.5
Outputs:
- solution: float32 [65536, 48], P(('feat', 'row'))
- residual: float32 [65536, 48], P(('feat', 'row'))
All inputs are finite; a program needn't handle non-finite values.
Results may differ from a plain program's by a relative error of at most 0.024.
Values may be sent and summed in bfloat16 or wider, within the bound.
A program may use at most 64 MiB of HBM per device.

v0:
```python
import jax
import jax.numpy as jnp
from jax import lax
from jax.sharding import PartitionSpec as P

ITERS = 3


def shards(design, targets, factor, weights, penalty):

    def normal_terms(rows_low):
        return lax.psum_scatter(
            lax.dot_general(
                design, rows_low, (((0,), (0,)), ((), ())), preferred_element_type=jnp.float32
            ),
            "row",
            scatter_dimension=0,
            tiled=True,
        )

    def precondition(residual):
        projected = jnp.dot(factor.T, residual, precision=lax.Precision.HIGHEST)
        projected = lax.psum(projected, ("row", "feat"))
        search = residual + jnp.dot(
            factor, weights[:, None] * projected, precision=lax.Precision.HIGHEST
        )
        inner = lax.psum(jnp.sum(residual * search, axis=0), ("row", "feat"))
        return (search, inner)

    residual = normal_terms(targets)
    solution = jnp.zeros_like(residual)
    search, inner = precondition(residual)
    direction = search
    for step_index in range(ITERS):
        dir_low = direction.astype(jnp.bfloat16)
        row_values = lax.psum(
            jnp.dot(
                design,
                lax.all_gather(dir_low, "row", axis=0, tiled=True),
                preferred_element_type=jnp.float32,
            ),
            "feat",
        )
        row_low = row_values.astype(jnp.bfloat16)
        dir_slice = direction
        local_part = jnp.sum(row_values * row_low.astype(jnp.float32), axis=0) / lax.axis_size(
            "feat"
        )
        local_part = local_part + penalty * jnp.sum(dir_slice * dir_slice, axis=0)
        curvature = lax.psum(local_part, ("row", "feat"))
        hessian_dir = normal_terms(row_low) + penalty[None, :] * dir_slice
        step_size = inner / curvature
        solution = solution + step_size[None, :] * dir_slice
        residual = residual - step_size[None, :] * hessian_dir
        if step_index + 1 < ITERS:
            search, inner_next = precondition(residual)
            direction = search + (inner_next / inner)[None, :] * direction
            inner = inner_next
    return (solution, residual)


def solution(mesh):
    return jax.shard_map(
        shards,
        mesh=mesh,
        in_specs=(P("row", "feat"), P("row", None), P(("feat", "row"), None), P(), P()),
        out_specs=(P(("feat", "row"), None), P(("feat", "row"), None)),
        check_vma=False,
    )
```

profile of v0, /device:TPU:0, one launch (start us, length us, event | category | flops | bytes accessed | tf_op | source)
XLA Modules:
  0.0 737.3 jit_solution(17198309492776830987)
XLA Ops:
  7.2 0.0 copy-start
  7.2 0.0 reduce-scatter.5.cloned.1.call-start
  7.2 4.7 fusion.13
  11.9 0.0 reduce-scatter.5.cloned.1.call-update
  12.0 0.0 copy-start.5
  12.0 0.0 all-gather.4.cloned.1.call-start
  12.0 77.5 %reduce-scatter.5.cloned.1.call-done = f32[2048,48]{0,1:T(8,128)} async-done(((f32[16384,48]{0,1:T(8,128)}), f32[2048,48]{0,1:T(8,128)}) %reduce-scatter.5.cloned.1.call-update) | async-done | bytes 393232 | tf_op jit(solution)/shard_map/reduce_scatter | solution.py:12
  89.6 0.0 copy-done
  89.6 4.5 convolution_bitcast_fusion.8
  94.1 40.7 %psum.84 = f32[256,48]{1,0:T(8,128)S(1)} all-reduce(f32[256,48]{1,0:T(8,128)S(1)} %convolution_bitcast_fusion.8), channel_id=1, replica_groups=mesh['row'=8,'feat'=4] {'row','feat'}, use_global_device_ids=true, to_apply=%region_1.0 | all-reduce | flops 12288 | bytes 98304 | tf_op jit(solution)/shard_map/psum | solution.py:23
  134.8 0.0 copy-done.5
  134.8 0.0 copy-done.3
  134.8 2.7 multiply_reduce_fusion.4
  137.5 0.0 copy-start.1
  137.5 0.0 all-gather.4.cloned.1.call-update
  137.6 0.0 reduce-scatter.7.cloned.1.call-start
  137.6 43.6 %all-gather.4.cloned.1.call-done = bf16[16384,48]{0,1:T(8,128)(2,1)} async-done(((bf16[2048,48]{0,1:T(8,128)(2,1)}), bf16[16384,48]{0,1:T(8,128)(2,1)}) %all-gather.4.cloned.1.call-update) | async-done | bytes 1572880 | tf_op jit(solution)/shard_map/all_gather | solution.py:39
  181.2 4.2 convolution_bitcast_fusion.11
  185.4 10.3 %psum.86 = f32[128,48]{0,1:T(8,128)S(1)} all-reduce(f32[128,48]{0,1:T(8,128)S(1)} %convolution_bitcast_fusion.11), channel_id=1, replica_groups=mesh['row'=8,'feat'=4] {'feat'}, use_global_device_ids=true, to_apply=%region_4.0 | all-reduce | flops 6144 | bytes 49152 | tf_op jit(solution)/shard_map/psum | solution.py:36
  195.7 4.5 convolution_bitcast_fusion.2
  200.2 0.0 reduce-scatter.7.cloned.1.call-update
  200.3 0.0 all-gather.6.cloned.1.call-start
  200.3 0.1 multiply_reduce_fusion.8
  200.4 0.5 copy-done.4
  200.9 40.9 %all-reduce = (f32[48]{0:T(128)S(1)}, f32[48]{0:T(128)S(1)}) all-reduce(f32[48]{0:T(128)S(1)} %get-tuple-element.3, f32[48]{0:T(128)S(1)} %multiply_add_fusion.5), channel_id=1, replica_groups=mesh['row'=8,'feat'=4] {'row','feat'}, use_global_device_ids=true, to_apply=%region_3.0 | all-reduce | flops 96 | bytes 768 | tf_op jit(solution)/shard_map/psum | solution.py:27
  241.8 33.1 %reduce-scatter.7.cloned.1.call-done = f32[2048,48]{0,1:T(8,128)} async-done(((f32[16384,48]{0,1:T(8,128)}), f32[2048,48]{0,1:T(8,128)}) %reduce-scatter.7.cloned.1.call-update) | async-done | bytes 393232 | tf_op jit(solution)/shard_map/reduce_scatter | solution.py:12
  274.9 1.1 multiply_subtract_fusion.2
  276.0 3.4 convolution_bitcast_fusion.7
  279.5 40.7 %psum.88 = f32[256,48]{1,0:T(8,128)S(1)} all-reduce(f32[256,48]{1,0:T(8,128)S(1)} %convolution_bitcast_fusion.7), channel_id=1, replica_groups=mesh['row'=8,'feat'=4] {'row','feat'}, use_global_device_ids=true, to_apply=%region_9.0 | all-reduce | flops 12288 | bytes 98304 | tf_op jit(solution)/shard_map/psum | solution.py:23
  320.2 2.8 multiply_reduce_fusion.3
  323.0 39.4 %psum.89 = f32[48]{0:T(128)S(1)} all-reduce(f32[48]{0:T(128)S(1)} %get-tuple-element.14), channel_id=1, replica_groups=mesh['row'=8,'feat'=4] {'row','feat'}, use_global_device_ids=true, to_apply=%region_11.0 | all-reduce | flops 48 | bytes 384 | tf_op jit(solution)/shard_map/psum | solution.py:27
  362.4 0.0 copy-done.1
  362.4 1.2 multiply_reduce_fusion.2
  363.7 0.7 convert_element_type.30
  364.4 0.0 all-gather.6.cloned.1.call-update
  364.4 0.0 reduce-scatter.9.cloned.1.call-start
  364.5 44.2 %all-gather.6.cloned.1.call-done = bf16[16384,48]{0,1:T(8,128)(2,1)} async-done(((bf16[2048,48]{0,1:T(8,128)(2,1)}), bf16[16384,48]{0,1:T(8,128)(2,1)}) %all-gather.6.cloned.1.call-update) | async-done | bytes 1572880 | tf_op jit(solution)/shard_map/all_gather | solution.py:39
  408.7 4.2 convolution_bitcast_fusion.10
  412.9 10.3 %psum.90 = f32[128,48]{0,1:T(8,128)S(1)} all-reduce(f32[128,48]{0,1:T(8,128)S(1)} %convolution_bitcast_fusion.10), channel_id=1, replica_groups=mesh['row'=8,'feat'=4] {'feat'}, use_global_device_ids=true, to_apply=%region_12.0 | all-reduce | flops 6144 | bytes 49152 | tf_op jit(solution)/shard_map/psum | solution.py:36
  423.2 4.5 convolution_bitcast_fusion.1
  427.7 0.0 reduce-scatter.9.cloned.1.call-update
  427.7 0.0 all-gather.8.cloned.1.call-start
  427.8 0.1 multiply_reduce_fusion.7
  427.9 41.2 %psum.91 = f32[48]{0:T(128)S(1)} all-reduce(f32[48]{0:T(128)S(1)} %multiply_add_fusion.4), channel_id=1, replica_groups=mesh['row'=8,'feat'=4] {'row','feat'}, use_global_device_ids=true, to_apply=%region_15.0 | all-reduce | flops 48 | bytes 384 | tf_op jit(solution)/shard_map/psum | solution.py:50
  469.1 33.4 %reduce-scatter.9.cloned.1.call-done = f32[2048,48]{0,1:T(8,128)} async-done(((f32[16384,48]{0,1:T(8,128)}), f32[2048,48]{0,1:T(8,128)}) %reduce-scatter.9.cloned.1.call-update) | async-done | bytes 393232 | tf_op jit(solution)/shard_map/reduce_scatter | solution.py:12
  502.5 1.1 multiply_subtract_fusion.1
  503.6 3.4 convolution_bitcast_fusion.6
  507.0 40.7 %psum.92 = f32[256,48]{1,0:T(8,128)S(1)} all-reduce(f32[256,48]{1,0:T(8,128)S(1)} %convolution_bitcast_fusion.6), channel_id=1, replica_groups=mesh['row'=8,'feat'=4] {'row','feat'}, use_global_device_ids=true, to_apply=%region_17.0 | all-reduce | flops 12288 | bytes 98304 | tf_op jit(solution)/shard_map/psum | solution.py:23
  547.7 2.0 multiply_reduce_fusion.1
  549.8 39.4 %psum.93 = f32[48]{0:T(128)S(1)} all-reduce(f32[48]{0:T(128)S(1)} %get-tuple-element.16), channel_id=1, replica_groups=mesh['row'=8,'feat'=4] {'row','feat'}, use_global_device_ids=true, to_apply=%region_19.0 | all-reduce | flops 48 | bytes 384 | tf_op jit(solution)/shard_map/psum | solution.py:27
  589.2 0.9 fusion.12
  590.1 0.0 all-gather.8.cloned.1.call-update
  590.1 0.0 reduce-scatter.11.cloned.1.call-start
  590.2 44.2 %all-gather.8.cloned.1.call-done = bf16[16384,48]{0,1:T(8,128)(2,1)} async-done(((bf16[2048,48]{0,1:T(8,128)(2,1)}), bf16[16384,48]{0,1:T(8,128)(2,1)}) %all-gather.8.cloned.1.call-update) | async-done | bytes 1572880 | tf_op jit(solution)/shard_map/all_gather | solution.py:39
  634.4 4.2 convolution_bitcast_fusion.9
  638.6 10.3 %psum.94 = f32[128,48]{0,1:T(8,128)S(1)} all-reduce(f32[128,48]{0,1:T(8,128)S(1)} %convolution_bitcast_fusion.9), channel_id=1, replica_groups=mesh['row'=8,'feat'=4] {'feat'}, use_global_device_ids=true, to_apply=%region_20.0 | all-reduce | flops 6144 | bytes 49152 | tf_op jit(solution)/shard_map/psum | solution.py:36
  648.9 4.5 convolution_bitcast_fusion
  653.4 0.0 reduce-scatter.11.cloned.1.call-update
  653.4 1.2 multiply_reduce_fusion
  654.6 0.1 multiply_reduce_fusion.6
  654.8 41.2 %psum.95 = f32[48]{0:T(128)S(1)} all-reduce(f32[48]{0:T(128)S(1)} %multiply_add_fusion.3), channel_id=1, replica_groups=mesh['row'=8,'feat'=4] {'row','feat'}, use_global_device_ids=true, to_apply=%region_23.0 | all-reduce | flops 48 | bytes 384 | tf_op jit(solution)/shard_map/psum | solution.py:50
  696.0 32.2 %reduce-scatter.11.cloned.1.call-done = f32[2048,48]{0,1:T(8,128)} async-done(((f32[16384,48]{0,1:T(8,128)}), f32[2048,48]{0,1:T(8,128)}) %reduce-scatter.11.cloned.1.call-update) | async-done | bytes 393232 | tf_op jit(solution)/shard_map/reduce_scatter | solution.py:12
  728.2 0.0 copy-done.2
  728.2 2.2 multiply_subtract_fusion
  (11 shorter events, 0.0 us)
Async XLA Ops:
  7.2 82.4 %copy-start = (f32[2048,256]{1,0:T(8,128)S(1)}, f32[2048,256]{1,0:T(8,128)}, u32[]{:S(2)}) copy-start(f32[2048,256]{1,0:T(8,128)} %param.7) | copy-start | bytes 6291460
  7.2 82.4 %reduce-scatter.5.cloned.1.call-start = ((), (), s32[]{:S(2)}) async-start(), calls=%async_computation.4 | async-start | bytes 3538944 | tf_op jit(solution)/shard_map/reduce_scatter | solution.py:12
  12.0 122.8 %copy-start.5 = (f32[256]{0:T(256)S(1)}, f32[256]{0:T(256)}, u32[]{:S(2)}) copy-start(f32[256]{0:T(256)} %param.8) | copy-start | bytes 3076
  12.0 169.2 %all-gather.4.cloned.1.call-start = ((), (), s32[]{:S(2)}) async-start(), calls=%async_computation.5 | async-start | bytes 1769472 | tf_op jit(solution)/shard_map/all_gather | solution.py:39
  89.6 45.2 %copy-start.3 = (f32[2048,48]{0,1:T(8,128)S(1)}, f32[2048,48]{0,1:T(8,128)}, u32[]{:S(2)}) copy-start(f32[2048,48]{0,1:T(8,128)} %reduce-scatter.5.cloned.1.call-done) | copy-start | bytes 1179652
  137.5 224.9 %copy-start.1 = (f32[2048,48]{0,1:T(8,128)}, f32[2048,48]{0,1:T(8,128)S(1)}, u32[]{:S(2)}) copy-start(f32[2048,48]{0,1:T(8,128)S(1)} %get-tuple-element.13) | copy-start | bytes 1179652
  137.6 137.4 %reduce-scatter.7.cloned.1.call-start = ((), (), s32[]{:S(2)}) async-start(), calls=%async_computation.6 | async-start | bytes 3538944 | tf_op jit(solution)/shard_map/reduce_scatter | solution.py:12
  200.2 0.7 copy-start.4
  200.3 208.4 %all-gather.6.cloned.1.call-start = ((), (), s32[]{:S(2)}) async-start(), calls=%async_computation.7 | async-start | bytes 1769472 | tf_op jit(solution)/shard_map/all_gather | solution.py:39
  364.4 138.0 %reduce-scatter.9.cloned.1.call-start = ((), (), s32[]{:S(2)}) async-start(), calls=%async_computation.8 | async-start | bytes 3538944 | tf_op jit(solution)/shard_map/reduce_scatter | solution.py:12
  427.7 206.7 %all-gather.8.cloned.1.call-start = ((), (), s32[]{:S(2)}) async-start(), calls=%async_computation.9 | async-start | bytes 1769472 | tf_op jit(solution)/shard_map/all_gather | solution.py:39
  590.1 138.1 %reduce-scatter.11.cloned.1.call-start = ((), (), s32[]{:S(2)}) async-start(), calls=%async_computation.10 | async-start | bytes 3538944 | tf_op jit(solution)/shard_map/reduce_scatter | solution.py:12
  653.4 74.8 %copy-start.2 = (f32[2048,48]{0,1:T(8,128)S(1)}, f32[2048,48]{0,1:T(8,128)}, u32[]{:S(2)}) copy-start(f32[2048,48]{0,1:T(8,128)} %copy-done.1) | copy-start | bytes 1179652
Sparse Core Ops, SparseCore 0:
  12.1 77.4 reduce-scatter.4
  137.7 43.4 all-gather.3
  200.4 74.5 reduce-scatter.6
  364.5 44.0 all-gather.5
  427.8 74.5 reduce-scatter.8
  590.2 44.1 all-gather.7
  653.6 74.6 reduce-scatter.10
where the time goes:
time: 739 us; the launch traced here: 737 us
  blocking collectives  355 us (48%)
  waiting for transfers between devices  308 us (42%)
  matrix products  49.8 us (7%)
  between operations  14.3 us (2%)
  other arithmetic  8.84 us (1%)
    reduce_scatter x4, waiting for transfers between devices, normal_terms(): lax.psum_scatter(lax.dot_general(design, rows_low, (((0,), (0,)), ((), ()...  176 us
    all_gather x3, waiting for transfers between devices, shards(): lax.all_gather(dir_low, 'row', axis=0, tiled=True)  132 us
    psum x3, blocking collectives, precondition(): projected = lax.psum(projected, ('row', 'feat'))  122 us
    psum x3, blocking collectives, precondition(): inner = lax.psum(jnp.sum(residual * search, axis=0), ('row', 'feat'))  120 us
    psum x2, blocking collectives, shards(): curvature = lax.psum(local_part, ('row', 'feat'))  82.4 us
    psum x3, blocking collectives, shards(): lax.psum(jnp.dot(design, lax.all_gather(dir_low, 'row', axis=0, tiled=Tru...  30.8 us
    dot_general x4, matrix products, normal_terms(): lax.dot_general(design, rows_low, (((0,), (0,)), ((), ())), preferred_ele...  18.3 us
  transfers between devices with their start and end apart: 7, of which 7 were waited for; matrix products, arithmetic and copies ran while one was open for 0% of the time, Pallas kernels for 0%

commit v1 on v0

--- a/solution.py
+++ b/solution.py
@@ -24,7 +24,8 @@
         search = residual + jnp.dot(
             factor, weights[:, None] * projected, precision=lax.Precision.HIGHEST
         )
-        inner = lax.psum(jnp.sum(residual * search, axis=0), ("row", "feat"))
+        partial = lax.psum(jnp.sum(residual * search, axis=0), "feat")
+        inner = lax.psum(partial, "row")
         return (search, inner)
 
     residual = normal_terms(targets)

time: 739 us -> 705 us (0.954)
  waiting for transfers between devices: 308 us -> 280 us
    psum x3 -> x5, blocking collectives: 120 us -> 73.5 us  [the longest x3 61.9 us: precondition(): inner = lax.psum(partial, 'row')]
    psum x2 -> x3, blocking collectives: 82.4 us -> 124 us  [shards(): curvature = lax.psum(local_part, ('row', 'feat'))]
    reduce_scatter x4, waiting for transfers between devices: 176 us -> 155 us  [normal_terms(): lax.psum_scatter(lax.dot_general(design, rows_low, (((0,), (0,)), ((), ()...]
where the time goes in v1:
time: 705 us; the launch traced here: 704 us
  blocking collectives  350 us (50%)
  waiting for transfers between devices  280 us (40%)
  matrix products  49.8 us (7%)
  between operations  14.3 us (2%)
  other arithmetic  8.85 us (1%)
    reduce_scatter x4, waiting for transfers between devices, normal_terms(): lax.psum_scatter(lax.dot_general(design, rows_low, (((0,), (0,)), ((), ()...  155 us
    all_gather x3, waiting for transfers between devices, shards(): lax.all_gather(dir_low, 'row', axis=0, tiled=True)  125 us
    psum x3, blocking collectives, shards(): curvature = lax.psum(local_part, ('row', 'feat'))  124 us
    psum x3, blocking collectives, precondition(): projected = lax.psum(projected, ('row', 'feat'))  122 us
    psum x3, blocking collectives, precondition(): inner = lax.psum(partial, 'row')  61.9 us
    psum x3, blocking collectives, shards(): lax.psum(jnp.dot(design, lax.all_gather(dir_low, 'row', axis=0, tiled=Tru...  30.8 us
    dot_general x4, matrix products, normal_terms(): lax.dot_general(design, rows_low, (((0,), (0,)), ((), ())), preferred_ele...  18.4 us
  transfers between devices with their start and end apart: 7, of which 7 were waited for; matrix products, arithmetic and copies ran while one was open for 0% of the time, Pallas kernels for 0%

profile of v1, /device:TPU:0, one launch (start us, length us, event | category | flops | bytes accessed | tf_op | source)
XLA Modules:
  0.0 703.9 jit_solution(8218213012270531250)
XLA Ops:
  7.2 0.0 copy-start
  7.2 0.0 reduce-scatter.5.cloned.1.call-start
  7.2 4.7 fusion.13
  11.9 0.0 reduce-scatter.5.cloned.1.call-update
  12.0 0.0 copy-start.5
  12.0 0.0 all-gather.4.cloned.1.call-start
  12.0 77.5 %reduce-scatter.5.cloned.1.call-done = f32[2048,48]{0,1:T(8,128)} async-done(((f32[16384,48]{0,1:T(8,128)}), f32[2048,48]{0,1:T(8,128)}) %reduce-scatter.5.cloned.1.call-update) | async-done | bytes 393232 | tf_op jit(solution)/shard_map/reduce_scatter | solution.py:12
  89.6 4.5 convolution_bitcast_fusion.8
  94.1 40.7 %psum.105 = f32[256,48]{1,0:T(8,128)S(1)} all-reduce(f32[256,48]{1,0:T(8,128)S(1)} %convolution_bitcast_fusion.8), channel_id=1, replica_groups=mesh['row'=8,'feat'=4] {'row','feat'}, use_global_device_ids=true, to_apply=%region_1.0 | all-reduce | flops 12288 | bytes 98304 | tf_op jit(solution)/shard_map/psum | solution.py:23
  134.8 0.0 copy-done.5
  134.8 0.0 copy-done.3
  134.8 2.7 multiply_reduce_fusion.4
  137.5 0.0 copy-start.1
  137.5 0.0 all-gather.4.cloned.1.call-update
  137.6 0.0 reduce-scatter.7.cloned.1.call-start
  137.6 43.6 %all-gather.4.cloned.1.call-done = bf16[16384,48]{0,1:T(8,128)(2,1)} async-done(((bf16[2048,48]{0,1:T(8,128)(2,1)}), bf16[16384,48]{0,1:T(8,128)(2,1)}) %all-gather.4.cloned.1.call-update) | async-done | bytes 1572880 | tf_op jit(solution)/shard_map/all_gather | solution.py:40
  181.2 4.2 convolution_bitcast_fusion.11
  185.4 10.3 %all-reduce = (f32[128,48]{0,1:T(8,128)S(1)}, f32[48]{0:T(128)S(1)}) all-reduce(f32[128,48]{0,1:T(8,128)S(1)} %convolution_bitcast_fusion.11, f32[48]{0:T(128)S(1)} %get-tuple-element.3), channel_id=1, replica_groups=mesh['row'=8,'feat'=4] {'feat'}, use_global_device_ids=true, to_apply=%region_5.0 | all-reduce | flops 6192 | bytes 49536 | tf_op jit(solution)/shard_map/psum | solution.py:37
  195.7 4.6 convolution_bitcast_fusion.2
  200.3 0.0 reduce-scatter.7.cloned.1.call-update
  200.3 0.0 all-gather.6.cloned.1.call-start
  200.3 0.1 multiply_reduce_fusion.8
  200.4 0.5 copy-done.4
  200.9 40.8 %psum.109 = f32[48]{0:T(128)S(1)} all-reduce(f32[48]{0:T(128)S(1)} %multiply_add_fusion.5), channel_id=1, replica_groups=mesh['row'=8,'feat'=4] {'row','feat'}, use_global_device_ids=true, to_apply=%region_8.0 | all-reduce | flops 48 | bytes 384 | tf_op jit(solution)/shard_map/psum | solution.py:51
  241.7 21.1 %psum.107 = f32[48]{0:T(128)S(1)} all-reduce(f32[48]{0:T(128)S(1)} %get-tuple-element.5), channel_id=1, replica_groups=mesh['row'=8,'feat'=4] {'row'}, use_global_device_ids=true, to_apply=%region_4.0 | all-reduce | flops 48 | bytes 384 | tf_op jit(solution)/shard_map/psum | solution.py:28
  262.8 12.3 %reduce-scatter.7.cloned.1.call-done = f32[2048,48]{0,1:T(8,128)} async-done(((f32[16384,48]{0,1:T(8,128)}), f32[2048,48]{0,1:T(8,128)}) %reduce-scatter.7.cloned.1.call-update) | async-done | bytes 393232 | tf_op jit(solution)/shard_map/reduce_scatter | solution.py:12
  275.1 1.1 multiply_subtract_fusion.2
  276.2 3.4 convolution_bitcast_fusion.7
  279.7 40.7 %psum.110 = f32[256,48]{1,0:T(8,128)S(1)} all-reduce(f32[256,48]{1,0:T(8,128)S(1)} %convolution_bitcast_fusion.7), channel_id=1, replica_groups=mesh['row'=8,'feat'=4] {'row','feat'}, use_global_device_ids=true, to_apply=%region_10.0 | all-reduce | flops 12288 | bytes 98304 | tf_op jit(solution)/shard_map/psum | solution.py:23
  320.4 2.8 multiply_reduce_fusion.3
  323.2 5.8 psum.111
  329.0 20.4 %psum.112 = f32[48]{0:T(128)S(1)} all-reduce(f32[48]{0:T(128)S(1)} %psum.111), channel_id=1, replica_groups=mesh['row'=8,'feat'=4] {'row'}, use_global_device_ids=true, to_apply=%region_13.0 | all-reduce | flops 48 | bytes 384 | tf_op jit(solution)/shard_map/psum | solution.py:28
  349.3 1.2 multiply_reduce_fusion.2
  350.6 0.7 convert_element_type.30
  351.3 0.0 all-gather.6.cloned.1.call-update
  351.3 0.0 reduce-scatter.9.cloned.1.call-start
  351.4 40.8 %all-gather.6.cloned.1.call-done = bf16[16384,48]{0,1:T(8,128)(2,1)} async-done(((bf16[2048,48]{0,1:T(8,128)(2,1)}), bf16[16384,48]{0,1:T(8,128)(2,1)}) %all-gather.6.cloned.1.call-update) | async-done | bytes 1572880 | tf_op jit(solution)/shard_map/all_gather | solution.py:40
  392.2 4.2 convolution_bitcast_fusion.10
  396.4 10.3 %psum.113 = f32[128,48]{0,1:T(8,128)S(1)} all-reduce(f32[128,48]{0,1:T(8,128)S(1)} %convolution_bitcast_fusion.10), channel_id=1, replica_groups=mesh['row'=8,'feat'=4] {'feat'}, use_global_device_ids=true, to_apply=%region_14.0 | all-reduce | flops 6144 | bytes 49152 | tf_op jit(solution)/shard_map/psum | solution.py:37
  406.7 4.5 convolution_bitcast_fusion.1
  411.2 0.0 reduce-scatter.9.cloned.1.call-update
  411.2 0.0 all-gather.8.cloned.1.call-start
  411.3 0.1 multiply_reduce_fusion.7
  411.4 41.3 %psum.114 = f32[48]{0:T(128)S(1)} all-reduce(f32[48]{0:T(128)S(1)} %multiply_add_fusion.4), channel_id=1, replica_groups=mesh['row'=8,'feat'=4] {'row','feat'}, use_global_device_ids=true, to_apply=%region_17.0 | all-reduce | flops 48 | bytes 384 | tf_op jit(solution)/shard_map/psum | solution.py:51
  452.7 33.1 %reduce-scatter.9.cloned.1.call-done = f32[2048,48]{0,1:T(8,128)} async-done(((f32[16384,48]{0,1:T(8,128)}), f32[2048,48]{0,1:T(8,128)}) %reduce-scatter.9.cloned.1.call-update) | async-done | bytes 393232 | tf_op jit(solution)/shard_map/reduce_scatter | solution.py:12
  485.8 1.1 multiply_subtract_fusion.1
  486.9 3.4 convolution_bitcast_fusion.6
  490.3 40.8 %psum.115 = f32[256,48]{1,0:T(8,128)S(1)} all-reduce(f32[256,48]{1,0:T(8,128)S(1)} %convolution_bitcast_fusion.6), channel_id=1, replica_groups=mesh['row'=8,'feat'=4] {'row','feat'}, use_global_device_ids=true, to_apply=%region_19.0 | all-reduce | flops 12288 | bytes 98304 | tf_op jit(solution)/shard_map/psum | solution.py:23
  531.1 2.0 multiply_reduce_fusion.1
  533.1 5.8 psum.116
  538.9 20.4 %psum.117 = f32[48]{0:T(128)S(1)} all-reduce(f32[48]{0:T(128)S(1)} %psum.116), channel_id=1, replica_groups=mesh['row'=8,'feat'=4] {'row'}, use_global_device_ids=true, to_apply=%region_22.0 | all-reduce | flops 48 | bytes 384 | tf_op jit(solution)/shard_map/psum | solution.py:28
  559.3 0.9 fusion.12
  560.2 0.0 all-gather.8.cloned.1.call-update
  560.3 0.0 reduce-scatter.11.cloned.1.call-start
  560.3 40.7 %all-gather.8.cloned.1.call-done = bf16[16384,48]{0,1:T(8,128)(2,1)} async-done(((bf16[2048,48]{0,1:T(8,128)(2,1)}), bf16[16384,48]{0,1:T(8,128)(2,1)}) %all-gather.8.cloned.1.call-update) | async-done | bytes 1572880 | tf_op jit(solution)/shard_map/all_gather | solution.py:40
  601.0 4.2 convolution_bitcast_fusion.9
  605.3 10.3 %psum.118 = f32[128,48]{0,1:T(8,128)S(1)} all-reduce(f32[128,48]{0,1:T(8,128)S(1)} %convolution_bitcast_fusion.9), channel_id=1, replica_groups=mesh['row'=8,'feat'=4] {'feat'}, use_global_device_ids=true, to_apply=%region_23.0 | all-reduce | flops 6144 | bytes 49152 | tf_op jit(solution)/shard_map/psum | solution.py:37
  615.5 4.5 convolution_bitcast_fusion
  620.1 0.0 reduce-scatter.11.cloned.1.call-update
  620.1 1.2 multiply_reduce_fusion
  621.3 0.1 multiply_reduce_fusion.6
  621.4 41.6 %psum.119 = f32[48]{0:T(128)S(1)} all-reduce(f32[48]{0:T(128)S(1)} %multiply_add_fusion.3), channel_id=1, replica_groups=mesh['row'=8,'feat'=4] {'row','feat'}, use_global_device_ids=true, to_apply=%region_26.0 | all-reduce | flops 48 | bytes 384 | tf_op jit(solution)/shard_map/psum | solution.py:51
  663.0 31.9 %reduce-scatter.11.cloned.1.call-done = f32[2048,48]{0,1:T(8,128)} async-done(((f32[16384,48]{0,1:T(8,128)}), f32[2048,48]{0,1:T(8,128)}) %reduce-scatter.11.cloned.1.call-update) | async-done | bytes 393232 | tf_op jit(solution)/shard_map/reduce_scatter | solution.py:12
  694.9 2.2 multiply_subtract_fusion
  (14 shorter events, 0.1 us)
Async XLA Ops:
  7.2 82.4 %copy-start = (f32[2048,256]{1,0:T(8,128)S(1)}, f32[2048,256]{1,0:T(8,128)}, u32[]{:S(2)}) copy-start(f32[2048,256]{1,0:T(8,128)} %param.7) | copy-start | bytes 6291460
  7.2 82.4 %reduce-scatter.5.cloned.1.call-start = ((), (), s32[]{:S(2)}) async-start(), calls=%async_computation.4 | async-start | bytes 3538944 | tf_op jit(solution)/shard_map/reduce_scatter | solution.py:12
  12.0 122.8 %copy-start.5 = (f32[256]{0:T(256)S(1)}, f32[256]{0:T(256)}, u32[]{:S(2)}) copy-start(f32[256]{0:T(256)} %param.8) | copy-start | bytes 3076
  12.0 169.2 %all-gather.4.cloned.1.call-start = ((), (), s32[]{:S(2)}) async-start(), calls=%async_computation.5 | async-start | bytes 1769472 | tf_op jit(solution)/shard_map/all_gather | solution.py:40
  89.6 45.2 %copy-start.3 = (f32[2048,48]{0,1:T(8,128)S(1)}, f32[2048,48]{0,1:T(8,128)}, u32[]{:S(2)}) copy-start(f32[2048,48]{0,1:T(8,128)} %reduce-scatter.5.cloned.1.call-done) | copy-start | bytes 1179652
  137.5 211.8 %copy-start.1 = (f32[2048,48]{0,1:T(8,128)}, f32[2048,48]{0,1:T(8,128)S(1)}, u32[]{:S(2)}) copy-start(f32[2048,48]{0,1:T(8,128)S(1)} %get-tuple-element.13) | copy-start | bytes 1179652
  137.6 137.6 %reduce-scatter.7.cloned.1.call-start = ((), (), s32[]{:S(2)}) async-start(), calls=%async_computation.6 | async-start | bytes 3538944 | tf_op jit(solution)/shard_map/reduce_scatter | solution.py:12
  200.3 0.7 copy-start.4
  200.3 191.9 %all-gather.6.cloned.1.call-start = ((), (), s32[]{:S(2)}) async-start(), calls=%async_computation.7 | async-start | bytes 1769472 | tf_op jit(solution)/shard_map/all_gather | solution.py:40
  351.3 134.5 %reduce-scatter.9.cloned.1.call-start = ((), (), s32[]{:S(2)}) async-start(), calls=%async_computation.8 | async-start | bytes 3538944 | tf_op jit(solution)/shard_map/reduce_scatter | solution.py:12
  411.2 189.8 %all-gather.8.cloned.1.call-start = ((), (), s32[]{:S(2)}) async-start(), calls=%async_computation.9 | async-start | bytes 1769472 | tf_op jit(solution)/shard_map/all_gather | solution.py:40
  560.3 134.6 %reduce-scatter.11.cloned.1.call-start = ((), (), s32[]{:S(2)}) async-start(), calls=%async_computation.10 | async-start | bytes 3538944 | tf_op jit(solution)/shard_map/reduce_scatter | solution.py:12
  620.1 74.8 %copy-start.2 = (f32[2048,48]{0,1:T(8,128)S(1)}, f32[2048,48]{0,1:T(8,128)}, u32[]{:S(2)}) copy-start(f32[2048,48]{0,1:T(8,128)} %copy-done.1) | copy-start | bytes 1179652
Sparse Core Ops, SparseCore 0:
  12.1 77.4 reduce-scatter.4
  137.7 43.4 all-gather.3
  200.4 74.6 reduce-scatter.6
  351.4 40.6 all-gather.5
  411.3 74.3 reduce-scatter.8
  560.4 40.6 all-gather.7
  620.2 74.5 reduce-scatter.10
